TPU v7x, 256 devices: a whole 4x4x8 slice. The times are simulated.
256 devices in a mesh: pipe: 2 (over core), slab: 8 (over x, z_hi), dp: 16 (over z_lo, y).
Axes of the slice: x: 4, y: 4, z: 8 (z_hi: 2, z_lo: 4; z = z_hi * 4 + z_lo), core: 2. Of those that a mesh axis runs over, the one named last changes fastest.
Arguments:
- saved_inputs: bfloat16 [2, 2, 16, 2, 16, 16, 512], P('pipe', None, 'dp', None, 'slab'), may hold values from -12 to 12
- loss_cotangent: bfloat16 [2, 16, 2, 16, 16, 512], P(None, 'dp', None, 'slab'), may hold values from -3 to 3
- upstream: bfloat16 [16, 2, 16, 16, 512], P('dp', None, 'slab'), may hold values from -3 to 3
- conv_weight: bfloat16 [2, 512, 13824], P('pipe', 'dp'), may hold values from -0.0546875 to 0.0546875
- adagn_table: bfloat16 [2, 1000, 1024], P('pipe'), may hold values from -3 to 3
- timesteps: int32 [3, 16], P(None, 'dp'), may hold values from 0 to 999
- frame_counts: int32 [3, 16], P(None, 'dp'), may hold values from 1 to 2
Outputs:
- input_grads: bfloat16 [2, 2, 16, 2, 16, 16, 512], P('pipe', None, 'dp', None, 'slab')
- weight_grad: float32 [2, 512, 13824], P('pipe', 'dp')
- embed_grad: float32 [2, 2, 16, 1024], P('pipe', None, 'dp')
All inputs are finite; a program needn't handle non-finite values.
Results may differ from a plain program's by a relative error of at most 0.015.
Values may be sent and summed in bfloat16 or wider, within the bound.
A program may use at most 128 MiB of HBM per device.

v0:
```python
import math
import jax
import jax.numpy as jnp
from jax import lax
from jax.sharding import PartitionSpec as P

GROUPS = 32
EPS = 1e-05


def extended(x, sides, width):
    for axis, dim in sides:
        devices, length = (lax.axis_size(axis), x.shape[dim])
        up = [(i, (i + 1) % devices) for i in range(devices - 1)]
        down = [(j, i) for i, j in up]
        last = lax.slice_in_dim(x, length - width, length, axis=dim)
        initial = lax.slice_in_dim(x, 0, width, axis=dim)
        before = lax.ppermute(last, axis, up)
        after = lax.ppermute(initial, axis, down)
        x = jnp.concatenate([before, x, after], axis=dim)
    return x


def shifted(block, axis, distance):
    devices = range(lax.axis_size(axis))
    route = [(i - distance, i) for i in devices if i - distance in devices]
    return lax.ppermute(block, axis, route)


def group_sums(values, groups):
    summed = jnp.sum(values.reshape(-1, values.shape[-1]), axis=0)
    return jnp.sum(summed.reshape(groups, -1), axis=1)


def silu_grad(preact):
    sigma = jax.nn.sigmoid(preact)
    return sigma * (1.0 + preact * (1.0 - sigma))


def hidden_of(values, mean_c, rstd_c, gain_row, bias_row, mask_now):
    normed = (values - mean_c) * rstd_c
    preact = normed * gain_row + bias_row
    activated = jax.nn.silu(preact) * mask_now[:, None, None, None]
    return (normed, preact, activated)


def norm_terms(moment_one, moment_two, count_now):
    mean_g = moment_one / count_now
    var_g = moment_two / count_now - mean_g * mean_g
    return (mean_g, lax.rsqrt(var_g + EPS))


def tap_stack(padded, frames, slab_rows, cells_wide, mirrored):
    slices = []
    for depth_at in range(3):
        for vertical in range(3):
            for across in range(3):
                if mirrored:
                    offsets = (2 - depth_at, 2 - vertical, 2 - across)
                else:
                    offsets = (depth_at, vertical, across)
                slices.append(
                    padded[
                        ...,
                        offsets[0] : offsets[0] + frames,
                        offsets[1] : offsets[1] + slab_rows,
                        offsets[2] : offsets[2] + cells_wide,
                        :,
                    ]
                )
    return jnp.stack(slices, 0)


def pad_cells(values):
    return jnp.pad(values, ((1, 1), (0, 0), (1, 1), (0, 0)))


def local(
    saved_inputs, loss_cotangent, upstream, conv_weight, adagn_table, timesteps, frame_counts
):
    section_index = lax.axis_index("pipe")
    slab_count = lax.axis_size("slab")
    replicas = lax.axis_size("dp")
    inputs = saved_inputs[0, :, 0]
    tick_count, frames, slab_rows, cells_wide, channels = inputs.shape
    groups = GROUPS
    per_group = channels // groups
    height_total = slab_rows * slab_count
    step_table = adagn_table[0]
    weight_local = conv_weight[0]
    steps_now = lax.dynamic_slice_in_dim(timesteps[:, 0], section_index, tick_count)
    counts_now = lax.dynamic_slice_in_dim(frame_counts[:, 0], section_index, tick_count)
    onehot = (
        steps_now[:, None] == jnp.arange(step_table.shape[0], dtype=jnp.int32)[None, :]
    ).astype(jnp.bfloat16)
    embedded = jnp.dot(onehot, step_table, preferred_element_type=jnp.float32)
    scales = 1.0 + embedded[:, :channels]
    shifts = embedded[:, channels:]
    frame_masks = (jnp.arange(frames, dtype=jnp.int32)[None, :] < counts_now[:, None]).astype(
        jnp.float32
    )
    valid_counts = counts_now.astype(jnp.float32) * float(height_total * cells_wide * per_group)
    weight_norm = 1.0 / math.sqrt(tick_count * replicas * frames * height_total * cells_wide)
    embed_norm = 1.0 / math.sqrt(frames * height_total * cells_wide)
    full_weight = lax.all_gather(weight_local, "dp", axis=0, tiled=True).reshape(
        channels, 27, channels
    )
    dx_list = []
    embed_list = []
    hidden_exts = []
    cotangents = []
    received = None
    for tick_index in range(tick_count):
        values = inputs[tick_index].astype(jnp.float32)
        masked = values * frame_masks[tick_index][:, None, None, None]
        part_one = group_sums(masked, groups)
        part_two = group_sums(masked * values, groups)
        moment_one, moment_two = lax.psum((part_one, part_two), "slab")
        count_now = valid_counts[tick_index]
        mean_g, rstd_g = norm_terms(moment_one, moment_two, count_now)
        mean_c = jnp.repeat(mean_g, per_group)
        rstd_c = jnp.repeat(rstd_g, per_group)
        mask_now = frame_masks[tick_index]
        normed, preact, activated = hidden_of(
            inputs[tick_index].astype(jnp.float32),
            mean_c,
            rstd_c,
            scales[tick_index],
            shifts[tick_index],
            mask_now,
        )
        hidden_ext = extended(activated.astype(jnp.bfloat16), (("slab", 1),), 1)
        hidden_exts.append(hidden_ext)
        incoming = upstream[0] if tick_index == 0 else received
        cotangent = jnp.where(section_index == 1, loss_cotangent[tick_index, 0], incoming)
        cot_rows = extended(cotangent, (("slab", 1),), 1)
        cot_pad = pad_cells(cot_rows)
        tap_slices = tap_stack(cot_pad, frames, slab_rows, cells_wide, True)
        upward = jnp.einsum(
            "tfrwo,oti->frwi", tap_slices, full_weight, preferred_element_type=jnp.float32
        )
        pre_grad = upward * silu_grad(preact) * mask_now[:, None, None, None]
        dnormed = pre_grad * scales[tick_index]
        part_a = group_sums(dnormed, groups)
        part_b = group_sums(dnormed * normed, groups)
        scale_part = jnp.sum(pre_grad * normed, axis=(0, 1, 2))
        shift_part = jnp.sum(pre_grad, axis=(0, 1, 2))
        sum_a, sum_b, scale_sum, shift_sum = lax.psum(
            (part_a, part_b, scale_part, shift_part), "slab"
        )
        branch = (
            rstd_c
            * (
                dnormed
                - jnp.repeat(sum_a / count_now, per_group)
                - normed * jnp.repeat(sum_b / count_now, per_group)
            )
            * mask_now[:, None, None, None]
        )
        result = (cotangent.astype(jnp.float32) + branch).astype(jnp.bfloat16)
        dx_list.append(result)
        embed_list.append(jnp.concatenate([scale_sum, shift_sum]) * embed_norm)
        cotangents.append(cotangent)
        if tick_index + 1 < tick_count:
            received = shifted(result, "pipe", -1)
    cot_all = jnp.stack(cotangents)
    shard_rows = weight_local.shape[0]
    hidden_all = jnp.stack([pad_cells(one_ext) for one_ext in hidden_exts])
    hidden_taps = tap_stack(hidden_all, frames, slab_rows, cells_wide, False)
    grad_term = jnp.einsum(
        "kfrwo,tkfrwi->oti", cot_all, hidden_taps, preferred_element_type=jnp.float32
    )
    grad_shard = lax.psum_scatter(
        (grad_term.reshape(lax.axis_size("dp") * shard_rows, -1) * weight_norm).astype(
            jnp.bfloat16
        ),
        "dp",
        scatter_dimension=0,
        tiled=True,
    ).astype(jnp.float32)
    weight_grad = lax.psum(grad_shard, "slab")
    input_grads = jnp.stack(dx_list)[None, :, None]
    embed_grad = jnp.stack(embed_list)[None, :, None]
    return (input_grads, weight_grad[None], embed_grad)


def solution(mesh):
    placed = (
        P("pipe", None, "dp", None, "slab", None, None),
        P(None, "dp", None, "slab", None, None),
        P("dp", None, "slab", None, None),
        P("pipe", "dp", None),
        P("pipe", None, None),
        P(None, "dp"),
        P(None, "dp"),
    )
    return jax.shard_map(
        local,
        mesh=mesh,
        in_specs=placed,
        out_specs=(
            P("pipe", None, "dp", None, "slab", None, None),
            P("pipe", "dp", None),
            P("pipe", None, "dp", None),
        ),
        check_vma=False,
    )
```

profile of v0, /device:TPU:8, one launch (start us, length us, event | category | flops | bytes accessed | tf_op | source)
XLA Modules:
  0.0 686.2 jit_solution(7426702432679894269)
XLA Ops:
  8.9 9.1 %collective-permute-start = (bf16[2,1,16,512]{3,2,1,0:T(8,128)(2,1)S(1)}, bf16[2,1,16,512]{3,2,1,0:T(8,128)(2,1)S(1)}, u32[]{:S(2)}, u32[]{:S(2)}) collective-permute-start(bf16[2,1,16,512]{3,2,1,0:T(8,128)(2,1)S(1)} %get-tuple-element.56), channel_id=1, source_target_pairs={{0,16},{16,32},{32,48},{48,64},{64,80},{80,96},{96,112},{1,17},{17... | collective-permute-start | bytes 98312 | tf_op jit(solution)/shard_map/ppermute | solution.py:18
  18.0 1.3 collective-permute-start.1
  21.5 32.6 %all-reduce.6 = (f32[32]{0:T(128)S(1)}, f32[32]{0:T(128)S(1)}) all-reduce(f32[32]{0:T(128)S(1)} %reduce_sum.183, f32[32]{0:T(128)S(1)} %reduce_sum.181), channel_id=1, replica_groups=mesh['pipe'=2,'slab'=8,'dp'=16] {'slab'}, use_global_device_ids=true, to_apply=%region_5.0 | all-reduce | flops 64 | bytes 512 | tf_op jit(solution)/shard_map/psum | solution.py:118
  74.7 94.1 %all-gather.3.cloned.1.call-done = bf16[1,512,13824]{2,1,0:T(8,128)(2,1)} async-done(((bf16[1,32,13824]{2,1,0:T(8,128)(2,1)}), bf16[1,512,13824]{2,1,0:T(8,128)(2,1)}) %all-gather.3.cloned.1.call-update) | async-done | bytes 14155792 | tf_op jit(solution)/shard_map/all_gather | solution.py:105
  168.8 18.7 %copy.101 = bf16[1,512,13824]{1,2,0:T(8,128)(2,1)} copy(bf16[1,512,13824]{2,1,0:T(8,128)(2,1)} %all-gather.3.cloned.1.call-done) | data formatting | bytes 28311552 | tf_op jit(solution)/shard_map/all_gather | solution.py:105
  187.5 10.0 %fusion.42 = (f32[512]{0:T(512)S(1)}, f32[512]{0:T(512)S(1)}, f32[512]{0:T(512)S(1)}, f32[512]{0:T(512)S(1)}, f32[2,2,16,512]{3,2,1,0:T(8,128)S(1)}) fusion(f32[512]{0:T(512)S(1)} %sub.59, f32[512]{0:T(512)S(1)} %mul.241, bf16[1,2,1,2,2,16,512]{6,5,4,3,2,1,0:T(8,128)(2,1)S(1)} %copy-done.3, f32[512]{0:T(512)S(1)} %bitcast.570, ...), kind=kOutput, calls=%fused_computation.194 | convolution fusion | flops 906655744 | bytes 16138248 | tf_op jit(solution)/shard_map/tfrwo,oti->frwi/dot_general | solution.py:139
  197.9 31.7 %all-reduce.5 = (f32[32]{0:T(128)S(1)}, f32[32]{0:T(128)S(1)}, f32[32]{0:T(128)S(1)}, f32[32]{0:T(128)S(1)}) all-reduce(f32[32]{0:T(128)S(1)} %reduce_sum.187, f32[32]{0:T(128)S(1)} %reduce_sum.185, f32[32]{0:T(128)S(1)} %reduce_sum.191, f32[32]{0:T(128)S(1)} %reduce_sum.189), channel_id=1, replica_groups=mesh['pipe'=2,'slab'=8,'dp'=16] {'slab'}, use_global_device_ids=true, to_apply=%region_11.12 | all-reduce | flops 128 | bytes 1024 | tf_op jit(solution)/shard_map/psum | solution.py:148
  230.7 1.3 collective-permute-start.2
  232.0 1.8 collective-permute-done.2
  235.1 1.3 collective-permute-start.4
  237.4 8.5 %collective-permute-start.5 = (bf16[2,1,16,512]{3,2,1,0:T(8,128)(2,1)S(1)}, bf16[2,1,16,512]{3,2,1,0:T(8,128)(2,1)S(1)}, u32[]{:S(2)}, u32[]{:S(2)}) collective-permute-start(bf16[2,1,16,512]{3,2,1,0:T(8,128)(2,1)S(1)} %get-tuple-element.52), channel_id=1, source_target_pairs={{0,16},{16,32},{32,48},{48,64},{64,80},{80,96},{96,112},{1,17},{17... | collective-permute-start | bytes 98312 | tf_op jit(solution)/shard_map/ppermute | solution.py:18
  245.9 1.3 collective-permute-start.6
  247.9 9.4 %fusion.6 = f32[2,2,16,512]{3,2,0,1:T(8,128)S(1)} fusion(bf16[512,27,512,1,1]{0,2,3,4,1:T(8,128)(2,1)} %bitcast.562, bf16[27,2,2,16,512]{4,3,2,1,0:T(8,128)(2,1)S(1)} %constant_dynamic-update-slice_fusion.27), kind=kOutput, calls=%fused_computation.63 | convolution fusion | flops 905969664 | bytes 16056320 | tf_op jit(solution)/shard_map/tfrwo,oti->frwi/dot_general | solution.py:139
  257.5 8.7 %collective-permute-start.7 = (bf16[2,1,16,512]{3,2,1,0:T(8,128)(2,1)S(1)}, bf16[2,1,16,512]{3,2,1,0:T(8,128)(2,1)S(1)}, u32[]{:S(2)}, u32[]{:S(2)}) collective-permute-start(bf16[2,1,16,512]{3,2,1,0:T(8,128)(2,1)S(1)} %get-tuple-element.50), channel_id=1, source_target_pairs={{0,16},{16,32},{32,48},{48,64},{64,80},{80,96},{96,112},{1,17},{17... | collective-permute-start | bytes 98312 | tf_op jit(solution)/shard_map/ppermute | solution.py:18
  266.2 1.3 collective-permute-start.8
  267.8 9.0 %collective-permute-done.8 = bf16[2,1,16,512]{3,2,1,0:T(8,128)(2,1)S(1)} collective-permute-done((bf16[2,1,16,512]{3,2,1,0:T(8,128)(2,1)S(1)}, bf16[2,1,16,512]{3,2,1,0:T(8,128)(2,1)S(1)}, u32[]{:S(2)}, u32[]{:S(2)}) %collective-permute-start.8) | collective-permute-done | bytes 32800 | tf_op jit(solution)/shard_map/ppermute | solution.py:19
  278.0 1.7 copy-done.2
  279.7 9.1 %fusion = bf16[512,27,512]{0,2,1:T(8,128)(2,1)} fusion(bf16[27,2,2,2,16,512]{5,4,3,2,1,0:T(8,128)(2,1)} %copy-done.2, bf16[1,2,2,16,512]{4,3,2,1,0:T(8,128)(2,1)S(1)} %bitcast.564, bf16[1,2,2,16,512]{4,3,2,1,0:T(8,128)(2,1)S(1)} %get-tuple-element.46), kind=kOutput, calls=%fused_computation.1 | convolution fusion | flops 1826160640 | bytes 17825792 | tf_op jit(solution)/shard_map/kfrwo,tkfrwi->oti/dot_general | solution.py:170
  288.8 18.6 %copy.108 = bf16[512,13824]{1,0:T(8,128)(2,1)} copy(bf16[512,13824]{0,1:T(8,128)(2,1)} %bitcast.563) | data formatting | bytes 28311552 | tf_op jit(solution)/shard_map/convert_element_type | solution.py:174
  307.5 193.0 %reduce-scatter.2.cloned.1.call-done = bf16[32,13824]{1,0:T(8,128)(2,1)} async-done(((bf16[512,13824]{1,0:T(8,128)(2,1)}), bf16[32,13824]{1,0:T(8,128)(2,1)}) %reduce-scatter.2.cloned.1.call-update) | async-done | bytes 884752 | tf_op jit(solution)/shard_map/reduce_scatter | solution.py:173
  500.5 2.5 bitcast_convert_fusion
  503.5 35.7 %all-reduce.4 = (f32[32]{0:T(128)S(1)}, f32[32]{0:T(128)S(1)}, f32[1,512]{1,0:T(1,128)S(1)}, f32[1,512]{1,0:T(1,128)S(1)}, f32[1,512]{1,0:T(1,128)S(1)}, /*index=5*/f32[1,512]{1,0:T(1,128)S(1)}) all-reduce(f32[32]{0:T(128)S(1)} %reduce_sum.195, f32[32]{0:T(128)S(1)} %reduce_sum.193, ...), channel_id=1, replica_groups=mesh['pipe'=2,'slab'=8,'dp'=16] {'slab'}, use_global_device_ids=true, to_apply=%region_23.24 | all-reduce | flops 2112 | bytes 16896 | tf_op jit(solution)/shard_map/psum | solution.py:148
  542.2 134.7 %all-reduce.9.cloned.1.call-done = f32[1,32,13824]{2,1,0:T(8,128)} async-done(((f32[1,32,13824]{2,1,0:T(8,128)}), f32[1,32,13824]{2,1,0:T(8,128)}) %all-reduce.9.cloned.1.call-update) | async-done | bytes 1769488 | tf_op jit(solution)/shard_map/psum | solution.py:181
  676.9 2.8 copy.209
  (171 shorter events, 33.5 us)
Async XLA Ops:
  7.2 48.2 %copy-start = (bf16[1,1000,1024]{2,1,0:T(8,128)(2,1)S(1)}, bf16[1,1000,1024]{2,1,0:T(8,128)(2,1)}, u32[]{:S(2)}) copy-start(bf16[1,1000,1024]{2,1,0:T(8,128)(2,1)} %param.11) | copy-start | bytes 6144004
  7.2 161.6 %all-gather.3.cloned.1.call-start = ((), (), s32[]{:S(2)}) async-start(), calls=%async_computation.3 | async-start | bytes 15040512 | tf_op jit(solution)/shard_map/all_gather | solution.py:105
  7.9 492.6 %reduce-scatter.2.cloned.1.call-start = ((), (), s32[]{:S(2)}) async-start(), calls=%async_computation.1 | async-start | bytes 15040512 | tf_op jit(solution)/shard_map/reduce_scatter | solution.py:173
  8.9 48.4 %collective-permute-start = (bf16[2,1,16,512]{3,2,1,0:T(8,128)(2,1)S(1)}, bf16[2,1,16,512]{3,2,1,0:T(8,128)(2,1)S(1)}, u32[]{:S(2)}, u32[]{:S(2)}) collective-permute-start(bf16[2,1,16,512]{3,2,1,0:T(8,128)(2,1)S(1)} %get-tuple-element.56), channel_id=1, source_target_pairs={{0,16},{16,32},{32,48},{48,64},{64,80},{80,96},{96,112},{1,17},{17... | collective-permute-start | bytes 98312 | tf_op jit(solution)/shard_map/ppermute | solution.py:18
  18.0 39.3 %collective-permute-start.1 = (bf16[2,1,16,512]{3,2,1,0:T(8,128)(2,1)S(1)}, bf16[2,1,16,512]{3,2,1,0:T(8,128)(2,1)S(1)}, u32[]{:S(2)}, u32[]{:S(2)}) collective-permute-start(bf16[2,1,16,512]{3,2,1,0:T(8,128)(2,1)S(1)} %get-tuple-element.57), channel_id=1, source_target_pairs={{16,0},{32,16},{48,32},{64,48},{80,64},{96,80},{112,96},{17,1},{33... | collective-permute-start | bytes 98312 | tf_op jit(solution)/shard_map/ppermute | solution.py:19
  55.4 10.3 %copy-start.4 = (bf16[2,1,2,2,16,512]{5,4,3,2,1,0:T(8,128)(2,1)S(1)}, bf16[2,1,2,2,16,512]{5,4,3,2,1,0:T(8,128)(2,1)}, u32[]{:S(2)}) copy-start(bf16[2,1,2,2,16,512]{5,4,3,2,1,0:T(8,128)(2,1)} %param.8) | copy-start | bytes 393220
  55.4 10.3 %copy-start.5 = (bf16[1,2,2,16,512]{4,3,2,1,0:T(8,128)(2,1)S(1)}, bf16[1,2,2,16,512]{4,3,2,1,0:T(8,128)(2,1)}, u32[]{:S(2)}) copy-start(bf16[1,2,2,16,512]{4,3,2,1,0:T(8,128)(2,1)} %param.9) | copy-start | bytes 196612
  74.7 112.8 %copy-start.3 = (bf16[1,2,1,2,2,16,512]{6,5,4,3,2,1,0:T(8,128)(2,1)S(1)}, bf16[1,2,1,2,2,16,512]{6,5,4,3,2,1,0:T(8,128)(2,1)}, u32[]{:S(2)}) copy-start(bf16[1,2,1,2,2,16,512]{6,5,4,3,2,1,0:T(8,128)(2,1)} %param.7) | copy-start | bytes 393220
  230.7 3.1 collective-permute-start.2
  233.8 13.3 %collective-permute-start.3 = (bf16[2,1,16,512]{3,2,1,0:T(8,128)(2,1)S(1)}, bf16[2,1,16,512]{3,2,1,0:T(8,128)(2,1)S(1)}, u32[]{:S(2)}, u32[]{:S(2)}) collective-permute-start(bf16[2,1,16,512]{3,2,1,0:T(8,128)(2,1)S(1)} %get-tuple-element.54), channel_id=1, source_target_pairs={{0,16},{16,32},{32,48},{48,64},{64,80},{80,96},{96,112},{1,17},{17... | collective-permute-start | bytes 98312 | tf_op jit(solution)/shard_map/ppermute | solution.py:18
  235.1 12.0 %collective-permute-start.4 = (bf16[2,1,16,512]{3,2,1,0:T(8,128)(2,1)S(1)}, bf16[2,1,16,512]{3,2,1,0:T(8,128)(2,1)S(1)}, u32[]{:S(2)}, u32[]{:S(2)}) collective-permute-start(bf16[2,1,16,512]{3,2,1,0:T(8,128)(2,1)S(1)} %get-tuple-element.55), channel_id=1, source_target_pairs={{16,0},{32,16},{48,32},{64,48},{80,64},{96,80},{112,96},{17,1},{33... | collective-permute-start | bytes 98312 | tf_op jit(solution)/shard_map/ppermute | solution.py:19
  237.4 30.1 %collective-permute-start.5 = (bf16[2,1,16,512]{3,2,1,0:T(8,128)(2,1)S(1)}, bf16[2,1,16,512]{3,2,1,0:T(8,128)(2,1)S(1)}, u32[]{:S(2)}, u32[]{:S(2)}) collective-permute-start(bf16[2,1,16,512]{3,2,1,0:T(8,128)(2,1)S(1)} %get-tuple-element.52), channel_id=1, source_target_pairs={{0,16},{16,32},{32,48},{48,64},{64,80},{80,96},{96,112},{1,17},{17... | collective-permute-start | bytes 98312 | tf_op jit(solution)/shard_map/ppermute | solution.py:18
  245.9 21.6 %collective-permute-start.6 = (bf16[2,1,16,512]{3,2,1,0:T(8,128)(2,1)S(1)}, bf16[2,1,16,512]{3,2,1,0:T(8,128)(2,1)S(1)}, u32[]{:S(2)}, u32[]{:S(2)}) collective-permute-start(bf16[2,1,16,512]{3,2,1,0:T(8,128)(2,1)S(1)} %get-tuple-element.53), channel_id=1, source_target_pairs={{16,0},{32,16},{48,32},{64,48},{80,64},{96,80},{112,96},{17,1},{33... | collective-permute-start | bytes 98312 | tf_op jit(solution)/shard_map/ppermute | solution.py:19
  257.5 10.3 %collective-permute-start.7 = (bf16[2,1,16,512]{3,2,1,0:T(8,128)(2,1)S(1)}, bf16[2,1,16,512]{3,2,1,0:T(8,128)(2,1)S(1)}, u32[]{:S(2)}, u32[]{:S(2)}) collective-permute-start(bf16[2,1,16,512]{3,2,1,0:T(8,128)(2,1)S(1)} %get-tuple-element.50), channel_id=1, source_target_pairs={{0,16},{16,32},{32,48},{48,64},{64,80},{80,96},{96,112},{1,17},{17... | collective-permute-start | bytes 98312 | tf_op jit(solution)/shard_map/ppermute | solution.py:18
  266.2 10.6 %collective-permute-start.8 = (bf16[2,1,16,512]{3,2,1,0:T(8,128)(2,1)S(1)}, bf16[2,1,16,512]{3,2,1,0:T(8,128)(2,1)S(1)}, u32[]{:S(2)}, u32[]{:S(2)}) collective-permute-start(bf16[2,1,16,512]{3,2,1,0:T(8,128)(2,1)S(1)} %get-tuple-element.51), channel_id=1, source_target_pairs={{16,0},{32,16},{48,32},{64,48},{80,64},{96,80},{112,96},{17,1},{33... | collective-permute-start | bytes 98312 | tf_op jit(solution)/shard_map/ppermute | solution.py:19
  278.0 1.7 copy-start.2
  307.5 369.4 %all-reduce.9.cloned.1.call-start = ((), (), s32[]{:S(2)}) async-start(), calls=%async_computation.2 | async-start | bytes 3538944 | tf_op jit(solution)/shard_map/psum | solution.py:181
  541.5 138.2 %copy-start.1 = (bf16[1,1000,1024]{2,1,0:T(8,128)(2,1)S(1)}, bf16[1,1000,1024]{2,1,0:T(8,128)(2,1)}, u32[]{:S(2)}) copy-start(bf16[1,1000,1024]{2,1,0:T(8,128)(2,1)} %param.11) | copy-start | bytes 6144004
Sparse Core Ops, SparseCore 0:
  9.8 158.9 all-gather.2
  307.6 192.8 reduce-scatter.1
  503.8 173.0 all-reduce.8
where the time goes:
time: 688 us; the launch traced here: 686 us
  waiting for transfers between devices  434 us (63%)
  blocking collectives  100 us (15%)
  local copies, waits for them, and re-layouts  61.5 us (9%)
  starting transfers between devices  34.2 us (5%)
  matrix products  28.9 us (4%)
  between operations  14.6 us (2%)
  other arithmetic  13.5 us (2%)
    reduce_scatter x1, waiting for transfers between devices, local(): lax.psum_scatter((grad_term.reshape(lax.axis_size('dp') * shard_rows, -1)...  193 us
    psum x1, waiting for transfers between devices, local(): weight_grad = lax.psum(grad_shard, 'slab')  135 us
    all_gather x1, waiting for transfers between devices, local(): lax.all_gather(weight_local, 'dp', axis=0, tiled=True)  94.1 us
    psum x2, blocking collectives, local(): lax.psum((part_a, part_b, scale_part, shift_part), 'slab')  67.4 us
    psum x1, blocking collectives, local(): moment_one, moment_two = lax.psum((part_one, part_two), 'slab')  32.6 us
    ppermute x4, starting transfers between devices, extended(): before = lax.ppermute(last, axis, up)  27.6 us
    unnamed x60, local copies, waits for them, and re-layouts  19.8 us
    dot_general x2, matrix products, local(): jnp.einsum('tfrwo,oti->frwi', tap_slices, full_weight, preferred_element_...  19.4 us
  transfers between devices with their start and end apart: 12, of which 6 were waited for; matrix products, arithmetic and copies ran while one was open for 6% of the time, Pallas kernels for 0%

commit v1 on v0

--- a/solution.py
+++ b/solution.py
@@ -102,9 +102,9 @@
     valid_counts = counts_now.astype(jnp.float32) * float(height_total * cells_wide * per_group)
     weight_norm = 1.0 / math.sqrt(tick_count * replicas * frames * height_total * cells_wide)
     embed_norm = 1.0 / math.sqrt(frames * height_total * cells_wide)
-    full_weight = lax.all_gather(weight_local, "dp", axis=0, tiled=True).reshape(
-        channels, 27, channels
-    )
+    full_weight = jnp.concatenate(
+        lax.all_to_all(jnp.stack([weight_local] * lax.axis_size("dp")), "dp", 0, 0), axis=0
+    ).reshape(channels, 27, channels)
     dx_list = []
     embed_list = []
     hidden_exts = []

time: 688 us -> 848 us (1.23)
  blocking collectives: 100 us -> 308 us
  waiting for transfers between devices: 434 us -> 341 us
  matrix products: 28.9 us -> 58 us
  local copies, waits for them, and re-layouts: 61.5 us -> 71 us
  starting transfers between devices: 34.2 us -> 42.7 us
    psum x1, blocking collectives: 32.6 us -> 244 us  [local(): moment_one, moment_two = lax.psum((part_one, part_two), 'slab')]
    all_gather x1 -> x0, waiting for transfers between devices: 94.1 us -> none  [local(): lax.all_gather(weight_local, 'dp', axis=0, tiled=True)]
    dot_general x2, matrix products: 19.4 us -> 48.5 us  [local(): jnp.einsum('tfrwo,oti->frwi', tap_slices, full_weight, preferred_element_...]
    another operation x0 -> x2, local copies, waits for them, and re-layouts: none -> 28.8 us  [the longest x1 21.1 us: local(): full_weight = jnp.concatenate(lax.all_to_all(jnp.stack([weight_local] * l...]
    all_gather x1 -> x0, local copies, waits for them, and re-layouts: 18.7 us -> none  [local(): lax.all_gather(weight_local, 'dp', axis=0, tiled=True)]
    all_to_all x0 -> x1, starting transfers between devices: none -> 9.14 us  [local(): lax.all_to_all(jnp.stack([weight_local] * lax.axis_size('dp')), 'dp', 0, 0)]
    unnamed x60 -> x64, local copies, waits for them, and re-layouts: 19.8 us -> 19.8 us
  transfers between devices with their start and end apart: 12 -> 12, of which waited for: 6 -> 4; matrix products, arithmetic and copies ran while one was open for 6% -> 6% of each run, Pallas kernels for 0% -> 0%
where the time goes in v1:
time: 848 us; the launch traced here: 847 us
  waiting for transfers between devices  341 us (40%)
  blocking collectives  308 us (36%)
  local copies, waits for them, and re-layouts  71 us (8%)
  matrix products  58 us (7%)
  starting transfers between devices  42.7 us (5%)
  between operations  14.9 us (2%)
  other arithmetic  11.1 us (1%)
    psum x1, blocking collectives, local(): moment_one, moment_two = lax.psum((part_one, part_two), 'slab')  244 us
    reduce_scatter x1, waiting for transfers between devices, local(): lax.psum_scatter((grad_term.reshape(lax.axis_size('dp') * shard_rows, -1)...  196 us
    psum x1, waiting for transfers between devices, local(): weight_grad = lax.psum(grad_shard, 'slab')  135 us
    psum x2, blocking collectives, local(): lax.psum((part_a, part_b, scale_part, shift_part), 'slab')  64.1 us
    dot_general x2, matrix products, local(): jnp.einsum('tfrwo,oti->frwi', tap_slices, full_weight, preferred_element_...  48.5 us
    ppermute x4, starting transfers between devices, extended(): before = lax.ppermute(last, axis, up)  26.6 us
    another operation x1, local copies, waits for them, and re-layouts, local(): full_weight = jnp.concatenate(lax.all_to_all(jnp.stack([weight_local] * l...  21.1 us
    unnamed x64, local copies, waits for them, and re-layouts  19.8 us
  transfers between devices with their start and end apart: 12, of which 4 were waited for; matrix products, arithmetic and copies ran while one was open for 6% of the time, Pallas kernels for 0%

profile of v1, /device:TPU:8, one launch (start us, length us, event | category | flops | bytes accessed | tf_op | source)
XLA Modules:
  0.0 846.9 jit_solution(2295259165947031657)
XLA Ops:
  7.2 7.7 stack.308
  14.9 9.1 %all-to-all-start = ((bf16[16,32,13824]{2,1,0:T(8,128)(2,1)}), bf16[16,32,13824]{2,1,0:T(8,128)(2,1)}, u32[]{:S(2)}, u32[]{:S(2)}) async-start(bf16[16,32,13824]{2,1,0:T(8,128)(2,1)} %stack.308), calls=%async_computation | async-start | bytes 28311552 | tf_op jit(solution)/shard_map/all_to_all | solution.py:106
  24.2 6.4 collective-permute-start
  30.6 1.3 collective-permute-start.1
  32.6 243.7 %all-reduce.6 = (f32[32]{0:T(128)S(1)}, f32[32]{0:T(128)S(1)}) all-reduce(f32[32]{0:T(128)S(1)} %reduce_sum.183, f32[32]{0:T(128)S(1)} %reduce_sum.181), channel_id=1, replica_groups=mesh['pipe'=2,'slab'=8,'dp'=16] {'slab'}, use_global_device_ids=true, to_apply=%region_5.0 | all-reduce | flops 64 | bytes 512 | tf_op jit(solution)/shard_map/psum | solution.py:118
  296.3 21.1 %reshape_reshape.3 = bf16[512,27,512]{2,1,0:T(8,128)(2,1)} reshape(bf16[16,32,13824]{2,1,0:T(8,128)(2,1)} %all-to-all-done) | data formatting | bytes 28311552 | tf_op jit(solution)/shard_map/reshape;reshape | solution.py:107
  317.4 24.5 %fusion.49 = (f32[512]{0:T(512)S(1)}, f32[512]{0:T(512)S(1)}, f32[512]{0:T(512)S(1)}, f32[512]{0:T(512)S(1)}, f32[2,2,16,512]{3,2,1,0:T(8,128)S(1)}) fusion(f32[512]{0:T(512)S(1)} %sub.59, f32[512]{0:T(512)S(1)} %mul.241, bf16[1,2,1,2,2,16,512]{6,5,4,3,2,1,0:T(8,128)(2,1)S(1)} %copy-done.3, f32[512]{0:T(512)S(1)} %bitcast.568, ...), kind=kOutput, calls=%fused_computation.196 | convolution fusion | flops 906655744 | bytes 16138248 | tf_op jit(solution)/shard_map/tfrwo,oti->frwi/dot_general | solution.py:139
  342.3 28.4 %all-reduce.5 = (f32[32]{0:T(128)S(1)}, f32[32]{0:T(128)S(1)}, f32[32]{0:T(128)S(1)}, f32[32]{0:T(128)S(1)}) all-reduce(f32[32]{0:T(128)S(1)} %reduce_sum.187, f32[32]{0:T(128)S(1)} %reduce_sum.185, f32[32]{0:T(128)S(1)} %reduce_sum.191, f32[32]{0:T(128)S(1)} %reduce_sum.189), channel_id=1, replica_groups=mesh['pipe'=2,'slab'=8,'dp'=16] {'slab'}, use_global_device_ids=true, to_apply=%region_11.12 | all-reduce | flops 128 | bytes 1024 | tf_op jit(solution)/shard_map/psum | solution.py:148
  373.1 1.8 collective-permute-done.2
  374.9 3.2 collective-permute-start.3
  380.5 8.5 collective-permute-start.5
  388.9 1.5 collective-permute-start.6
  391.2 24.0 %fusion.1 = f32[2,2,16,512,1]{3,2,0,1,4:T(8,128)S(1)} fusion(bf16[512,27,512,1,1]{2,1,0,4,3:T(8,128)(2,1)} %bitcast.559, bf16[27,2,2,16,512]{4,3,2,1,0:T(8,128)(2,1)S(1)} %constant_dynamic-update-slice_fusion.27), kind=kOutput, calls=%fused_computation.2 | convolution fusion | flops 905969664 | bytes 16056320 | tf_op jit(solution)/shard_map/tfrwo,oti->frwi/dot_general | solution.py:139
  415.4 8.5 collective-permute-start.7
  423.8 1.6 collective-permute-start.8
  425.5 8.4 collective-permute-done.8
  435.1 1.7 copy-done.2
  436.8 9.1 %fusion = bf16[512,27,512]{0,2,1:T(8,128)(2,1)} fusion(bf16[27,2,2,2,16,512]{5,4,3,2,1,0:T(8,128)(2,1)} %copy-done.2, bf16[1,2,2,16,512]{4,3,2,1,0:T(8,128)(2,1)S(1)} %bitcast.560, bf16[1,2,2,16,512]{4,3,2,1,0:T(8,128)(2,1)S(1)} %get-tuple-element.43), kind=kOutput, calls=%fused_computation.1 | convolution fusion | flops 1826160640 | bytes 17825792 | tf_op jit(solution)/shard_map/kfrwo,tkfrwi->oti/dot_general | solution.py:170
  445.9 18.6 %copy.72 = bf16[512,13824]{1,0:T(8,128)(2,1)} copy(bf16[512,13824]{0,1:T(8,128)(2,1)} %bitcast.557) | data formatting | bytes 28311552 | tf_op jit(solution)/shard_map/convert_element_type | solution.py:174
  464.6 196.1 %reduce-scatter.2.cloned.1.call-done = bf16[32,13824]{1,0:T(8,128)(2,1)} async-done(((bf16[512,13824]{1,0:T(8,128)(2,1)}), bf16[32,13824]{1,0:T(8,128)(2,1)}) %reduce-scatter.2.cloned.1.call-update) | async-done | bytes 884752 | tf_op jit(solution)/shard_map/reduce_scatter | solution.py:173
  660.7 2.5 bitcast_convert_fusion
  663.6 35.7 %all-reduce.4 = (f32[32]{0:T(128)S(1)}, f32[32]{0:T(128)S(1)}, f32[1,512]{1,0:T(1,128)S(1)}, f32[1,512]{1,0:T(1,128)S(1)}, f32[1,512]{1,0:T(1,128)S(1)}, /*index=5*/f32[1,512]{1,0:T(1,128)S(1)}) all-reduce(f32[32]{0:T(128)S(1)} %reduce_sum.195, f32[32]{0:T(128)S(1)} %reduce_sum.193, ...), channel_id=1, replica_groups=mesh['pipe'=2,'slab'=8,'dp'=16] {'slab'}, use_global_device_ids=true, to_apply=%region_23.24 | all-reduce | flops 2112 | bytes 16896 | tf_op jit(solution)/shard_map/psum | solution.py:148
  702.3 134.9 %all-reduce.9.cloned.1.call-done = f32[1,32,13824]{2,1,0:T(8,128)} async-done(((f32[1,32,13824]{2,1,0:T(8,128)}), f32[1,32,13824]{2,1,0:T(8,128)}) %all-reduce.9.cloned.1.call-update) | async-done | bytes 1769488 | tf_op jit(solution)/shard_map/psum | solution.py:181
  837.3 2.8 copy.189
  (175 shorter events, 30.8 us)
Async XLA Ops:
  7.2 269.8 %copy-start = (bf16[1,1000,1024]{2,1,0:T(8,128)(2,1)S(1)}, bf16[1,1000,1024]{2,1,0:T(8,128)(2,1)}, u32[]{:S(2)}) copy-start(bf16[1,1000,1024]{2,1,0:T(8,128)(2,1)} %param.11) | copy-start | bytes 6144004
  14.9 9.2 %copy-start.4 = (bf16[2,1,2,2,16,512]{5,4,3,2,1,0:T(8,128)(2,1)S(1)}, bf16[2,1,2,2,16,512]{5,4,3,2,1,0:T(8,128)(2,1)}, u32[]{:S(2)}) copy-start(bf16[2,1,2,2,16,512]{5,4,3,2,1,0:T(8,128)(2,1)} %param.8) | copy-start | bytes 393220
  14.9 9.2 %copy-start.5 = (bf16[1,2,2,16,512]{4,3,2,1,0:T(8,128)(2,1)S(1)}, bf16[1,2,2,16,512]{4,3,2,1,0:T(8,128)(2,1)}, u32[]{:S(2)}) copy-start(bf16[1,2,2,16,512]{4,3,2,1,0:T(8,128)(2,1)} %param.9) | copy-start | bytes 196612
  14.9 17.0 %copy-start.6 = (s32[3,1]{0,1:T(1,128)S(1)}, s32[3,1]{0,1:T(1,128)}, u32[]{:S(2)}) copy-start(s32[3,1]{0,1:T(1,128)} %param.13) | copy-start | bytes 40
  14.9 17.1 %copy-start.3 = (bf16[1,2,1,2,2,16,512]{6,5,4,3,2,1,0:T(8,128)(2,1)S(1)}, bf16[1,2,1,2,2,16,512]{6,5,4,3,2,1,0:T(8,128)(2,1)}, u32[]{:S(2)}) copy-start(bf16[1,2,1,2,2,16,512]{6,5,4,3,2,1,0:T(8,128)(2,1)} %param.7) | copy-start | bytes 393220
  14.9 261.4 %copy-start.7 = (s32[3,1]{0,1:T(1,128)S(1)}, s32[3,1]{0,1:T(1,128)}, u32[]{:S(2)}) copy-start(s32[3,1]{0,1:T(1,128)} %param.12) | copy-start | bytes 40
  14.9 281.4 %all-to-all-start = ((bf16[16,32,13824]{2,1,0:T(8,128)(2,1)}), bf16[16,32,13824]{2,1,0:T(8,128)(2,1)}, u32[]{:S(2)}, u32[]{:S(2)}) async-start(bf16[16,32,13824]{2,1,0:T(8,128)(2,1)} %stack.308), calls=%async_computation | async-start | bytes 28311552 | tf_op jit(solution)/shard_map/all_to_all | solution.py:106
  24.1 636.6 %reduce-scatter.2.cloned.1.call-start = ((), (), s32[]{:S(2)}) async-start(), calls=%async_computation.2 | async-start | bytes 15040512 | tf_op jit(solution)/shard_map/reduce_scatter | solution.py:173
  24.2 254.7 %collective-permute-start = (bf16[2,1,16,512]{3,2,1,0:T(8,128)(2,1)S(1)}, bf16[2,1,16,512]{3,2,1,0:T(8,128)(2,1)S(1)}, u32[]{:S(2)}, u32[]{:S(2)}) collective-permute-start(bf16[2,1,16,512]{3,2,1,0:T(8,128)(2,1)S(1)} %get-tuple-element.53), channel_id=1, source_target_pairs={{0,16},{16,32},{32,48},{48,64},{64,80},{80,96},{96,112},{1,17},{17... | collective-permute-start | bytes 98312 | tf_op jit(solution)/shard_map/ppermute | solution.py:18
  30.6 248.3 %collective-permute-start.1 = (bf16[2,1,16,512]{3,2,1,0:T(8,128)(2,1)S(1)}, bf16[2,1,16,512]{3,2,1,0:T(8,128)(2,1)S(1)}, u32[]{:S(2)}, u32[]{:S(2)}) collective-permute-start(bf16[2,1,16,512]{3,2,1,0:T(8,128)(2,1)S(1)} %get-tuple-element.54), channel_id=1, source_target_pairs={{16,0},{32,16},{48,32},{64,48},{80,64},{96,80},{112,96},{17,1},{33... | collective-permute-start | bytes 98312 | tf_op jit(solution)/shard_map/ppermute | solution.py:19
  371.8 3.1 collective-permute-start.2
  374.9 15.5 %collective-permute-start.3 = (bf16[2,1,16,512]{3,2,1,0:T(8,128)(2,1)S(1)}, bf16[2,1,16,512]{3,2,1,0:T(8,128)(2,1)S(1)}, u32[]{:S(2)}, u32[]{:S(2)}) collective-permute-start(bf16[2,1,16,512]{3,2,1,0:T(8,128)(2,1)S(1)} %get-tuple-element.51), channel_id=1, source_target_pairs={{0,16},{16,32},{32,48},{48,64},{64,80},{80,96},{96,112},{1,17},{17... | collective-permute-start | bytes 98312 | tf_op jit(solution)/shard_map/ppermute | solution.py:18
  378.2 12.3 %collective-permute-start.4 = (bf16[2,1,16,512]{3,2,1,0:T(8,128)(2,1)S(1)}, bf16[2,1,16,512]{3,2,1,0:T(8,128)(2,1)S(1)}, u32[]{:S(2)}, u32[]{:S(2)}) collective-permute-start(bf16[2,1,16,512]{3,2,1,0:T(8,128)(2,1)S(1)} %get-tuple-element.52), channel_id=1, source_target_pairs={{16,0},{32,16},{48,32},{64,48},{80,64},{96,80},{112,96},{17,1},{33... | collective-permute-start | bytes 98312 | tf_op jit(solution)/shard_map/ppermute | solution.py:19
  380.5 44.9 %collective-permute-start.5 = (bf16[2,1,16,512]{3,2,1,0:T(8,128)(2,1)S(1)}, bf16[2,1,16,512]{3,2,1,0:T(8,128)(2,1)S(1)}, u32[]{:S(2)}, u32[]{:S(2)}) collective-permute-start(bf16[2,1,16,512]{3,2,1,0:T(8,128)(2,1)S(1)} %get-tuple-element.49), channel_id=1, source_target_pairs={{0,16},{16,32},{32,48},{48,64},{64,80},{80,96},{96,112},{1,17},{17... | collective-permute-start | bytes 98312 | tf_op jit(solution)/shard_map/ppermute | solution.py:18
  388.9 36.5 %collective-permute-start.6 = (bf16[2,1,16,512]{3,2,1,0:T(8,128)(2,1)S(1)}, bf16[2,1,16,512]{3,2,1,0:T(8,128)(2,1)S(1)}, u32[]{:S(2)}, u32[]{:S(2)}) collective-permute-start(bf16[2,1,16,512]{3,2,1,0:T(8,128)(2,1)S(1)} %get-tuple-element.50), channel_id=1, source_target_pairs={{16,0},{32,16},{48,32},{64,48},{80,64},{96,80},{112,96},{17,1},{33... | collective-permute-start | bytes 98312 | tf_op jit(solution)/shard_map/ppermute | solution.py:19
  415.4 10.1 %collective-permute-start.7 = (bf16[2,1,16,512]{3,2,1,0:T(8,128)(2,1)S(1)}, bf16[2,1,16,512]{3,2,1,0:T(8,128)(2,1)S(1)}, u32[]{:S(2)}, u32[]{:S(2)}) collective-permute-start(bf16[2,1,16,512]{3,2,1,0:T(8,128)(2,1)S(1)} %get-tuple-element.47), channel_id=1, source_target_pairs={{0,16},{16,32},{32,48},{48,64},{64,80},{80,96},{96,112},{1,17},{17... | collective-permute-start | bytes 98312 | tf_op jit(solution)/shard_map/ppermute | solution.py:18
  423.8 10.1 %collective-permute-start.8 = (bf16[2,1,16,512]{3,2,1,0:T(8,128)(2,1)S(1)}, bf16[2,1,16,512]{3,2,1,0:T(8,128)(2,1)S(1)}, u32[]{:S(2)}, u32[]{:S(2)}) collective-permute-start(bf16[2,1,16,512]{3,2,1,0:T(8,128)(2,1)S(1)} %get-tuple-element.48), channel_id=1, source_target_pairs={{16,0},{32,16},{48,32},{64,48},{80,64},{96,80},{112,96},{17,1},{33... | collective-permute-start | bytes 98312 | tf_op jit(solution)/shard_map/ppermute | solution.py:19
  435.0 1.7 copy-start.2
  464.6 372.7 %all-reduce.9.cloned.1.call-start = ((), (), s32[]{:S(2)}) async-start(), calls=%async_computation.3 | async-start | bytes 3538944 | tf_op jit(solution)/shard_map/psum | solution.py:181
  701.6 138.4 %copy-start.1 = (bf16[1,1000,1024]{2,1,0:T(8,128)(2,1)S(1)}, bf16[1,1000,1024]{2,1,0:T(8,128)(2,1)}, u32[]{:S(2)}) copy-start(bf16[1,1000,1024]{2,1,0:T(8,128)(2,1)} %param.11) | copy-start | bytes 6144004
Sparse Core Ops, SparseCore 0:
  464.7 195.9 reduce-scatter.1
  663.9 173.2 all-reduce.8
